TPU v7x, 256 devices: a whole 4x4x8 slice. The times are simulated.
256 devices in a mesh: row: 32 (over z, y), col: 8 (over x, core).
Axes of the slice: x: 4, y: 4, z: 8, core: 2. Of those that a mesh axis runs over, the one named last changes fastest.
Arguments:
- anc_factor: float32 [32768, 8192], P('row', 'col'), may hold values from -0.046875 to 0.046875
- anc_solution: float32 [128, 49152], P('col', 'row'), may hold values from -6 to 6
- slot_row: int32 [32768], P('row'), may hold values from 0 to 1535, as said below
- tile_count: int32 [32], P('row'), may hold values from 2 to 8, as said below
- lower_factor: float32 [8, 1024, 8192], P(None, 'row', 'col'), may hold values from -0.109375 to 0.109375
- diag_inverse: float32 [8, 1024, 1024], P('col'), may hold values from -1.5 to 1.5, as said below
- rhs: float32 [128, 8192], P('row', 'col'), may hold values from -6 to 6
Outputs:
- solution: float32 [128, 8192], P('row', 'col')
Inputs may be any that keep to these rules, and one draw needn't show every extreme that they name: `slot_row`: within each aligned block of 1024 entries the values are distinct, and some block holds 1535. `tile_count`: some entry equals 8 in every draw. Each block diag_inverse[t] is lower triangular with a positive diagonal.
All inputs are finite; a program needn't handle non-finite values.
Results may differ from a plain program's by a relative error of at most 0.0001.
Values sent between devices are 32-bit elements; how exact they have to be, the bound alone decides.
No kernel may reach another device: no remote copies, remote signals or barrier semaphores. Data moves between devices by JAX's collectives and lax.ppermute only.
A program may use at most 64 MiB of HBM per device.

v0:
```python
import jax
import jax.numpy as jnp
from jax import lax
from jax.sharding import PartitionSpec as P

TILE = 128


def broadcast(array, axis, root):
    mine = lax.axis_index(axis) == root
    return lax.psum(jnp.where(mine, array, jnp.zeros_like(array)), axis)


def on_device(anc_factor, anc_solution, slot_row, tile_count, lower_factor, diag_inverse, rhs):
    highest = lax.Precision.HIGHEST
    column_index = lax.axis_index("col")
    panels = lower_factor.shape[0]
    rows_local = lower_factor.shape[1]
    slot_total = slot_row.shape[0]
    alive_mask = (jnp.arange(slot_total) < tile_count[0] * TILE).astype(jnp.float32)
    chosen = (
        jnp.take(lax.all_gather(anc_solution, "col", axis=0, tiled=True), slot_row, axis=1)
        * alive_mask[None, :]
    )
    ancestor_term = jnp.dot(
        chosen, anc_factor, precision=highest, preferred_element_type=jnp.float32
    )
    reduced = rhs - lax.psum_scatter(ancestor_term, "row", scatter_dimension=0, tiled=True)
    pending = jnp.zeros_like(reduced)
    result = jnp.zeros_like(reduced)
    panel_mask = (jnp.arange(panels) > column_index).astype(jnp.float32)
    lower_masked = lower_factor * panel_mask[:, None, None]
    lower_flat = lower_masked.reshape(panels * rows_local, lower_factor.shape[2])
    all_rhs = anc_solution.shape[0] * lax.axis_size("col")
    known_rows = jnp.zeros((all_rhs, panels * rows_local), jnp.float32)
    for target in range(panels - 1, -1, -1):
        if target < panels - 1:
            partial_sum = jnp.dot(
                known_rows, lower_flat, precision=highest, preferred_element_type=jnp.float32
            )
            pending = lax.psum_scatter(partial_sum, "row", scatter_dimension=0, tiled=True)
        solved = jnp.dot(
            reduced - pending,
            diag_inverse[0],
            precision=highest,
            preferred_element_type=jnp.float32,
        )
        result = jnp.where(column_index == target, solved, result)
        if target > 0:
            spread_rows = lax.all_to_all(solved, "row", split_axis=1, concat_axis=0, tiled=True)
            owner_rows = broadcast(spread_rows, "col", target)
            known_rows = known_rows.at[:, target * rows_local : (target + 1) * rows_local].set(
                owner_rows
            )
    return result


def solution(mesh):
    in_specs = (
        P("row", "col"),
        P("col", "row"),
        P("row"),
        P("row"),
        P(None, "row", "col"),
        P("col", None, None),
        P("row", "col"),
    )
    out_specs = P("row", "col")
    return jax.shard_map(
        on_device, mesh=mesh, in_specs=in_specs, out_specs=out_specs, check_vma=False
    )
```

profile of v0, /device:TPU:2, one launch (start us, length us, event | category | flops | bytes accessed | tf_op | source)
XLA Modules:
  0.0 1519.6 jit_solution(10085805310040251316)
XLA Ops:
  8.6 13.7 all_gather.3
  22.5 2.8 gather_fusion
  25.3 5.8 fusion.19
  32.4 150.3 %all-reduce.18.cloned.1.call-done = f32[128,1024]{1,0:T(8,128)} async-done(((f32[128,1024]{1,0:T(8,128)}), f32[128,1024]{1,0:T(8,128)}) %all-reduce.18.cloned.1.call-update) | async-done | bytes 524304
  183.5 4.3 fusion.14
  188.7 5.6 all-to-all-start
  194.5 9.4 all-to-all-done
  205.4 21.0 %psum.49 = f32[128,32]{1,0:T(8,128)S(1)} all-reduce(f32[128,32]{1,0:T(8,128)S(1)} %bitcast.107), channel_id=1, replica_groups=mesh['row'=32,'col'=8] {'col'}, use_global_device_ids=true, to_apply=%region_1.2 | all-reduce | flops 4096 | bytes 32768 | tf_op jit(solution)/shard_map/psum | solution.py:11
  226.3 1.5 fusion.25
  227.9 144.0 %all-reduce.20.cloned.1.call-done = f32[128,1024]{1,0:T(8,128)} async-done(((f32[128,1024]{1,0:T(8,128)}), f32[128,1024]{1,0:T(8,128)}) %all-reduce.20.cloned.1.call-update) | async-done | bytes 524304
  371.9 4.3 fusion.12
  377.1 5.6 all-to-all-start.1
  383.5 8.8 all-to-all-done.1
  393.2 21.2 %psum.50 = f32[128,32]{1,0:T(8,128)S(1)} all-reduce(f32[128,32]{1,0:T(8,128)S(1)} %bitcast.108), channel_id=1, replica_groups=mesh['row'=32,'col'=8] {'col'}, use_global_device_ids=true, to_apply=%region_4.5 | all-reduce | flops 4096 | bytes 32768 | tf_op jit(solution)/shard_map/psum | solution.py:11
  415.7 1.5 fusion.38
  417.2 144.0 %all-reduce.22.cloned.1.call-done = f32[128,1024]{1,0:T(8,128)} async-done(((f32[128,1024]{1,0:T(8,128)}), f32[128,1024]{1,0:T(8,128)}) %all-reduce.22.cloned.1.call-update) | async-done | bytes 524304
  561.2 4.3 fusion.10
  566.4 5.6 all-to-all-start.2
  572.7 8.9 all-to-all-done.2
  582.5 21.0 %psum.51 = f32[128,32]{1,0:T(8,128)S(1)} all-reduce(f32[128,32]{1,0:T(8,128)S(1)} %bitcast.109), channel_id=1, replica_groups=mesh['row'=32,'col'=8] {'col'}, use_global_device_ids=true, to_apply=%region_7.8 | all-reduce | flops 4096 | bytes 32768 | tf_op jit(solution)/shard_map/psum | solution.py:11
  604.8 1.5 fusion.39
  606.4 144.0 %all-reduce.24.cloned.1.call-done = f32[128,1024]{1,0:T(8,128)} async-done(((f32[128,1024]{1,0:T(8,128)}), f32[128,1024]{1,0:T(8,128)}) %all-reduce.24.cloned.1.call-update) | async-done | bytes 524304
  750.4 4.3 fusion.8
  755.5 5.6 all-to-all-start.3
  761.8 8.9 all-to-all-done.3
  771.6 21.0 %psum.52 = f32[128,32]{1,0:T(8,128)S(1)} all-reduce(f32[128,32]{1,0:T(8,128)S(1)} %bitcast.110), channel_id=1, replica_groups=mesh['row'=32,'col'=8] {'col'}, use_global_device_ids=true, to_apply=%region_10.11 | all-reduce | flops 4096 | bytes 32768 | tf_op jit(solution)/shard_map/psum | solution.py:11
  793.7 1.5 fusion.40
  795.3 144.0 %all-reduce.26.cloned.1.call-done = f32[128,1024]{1,0:T(8,128)} async-done(((f32[128,1024]{1,0:T(8,128)}), f32[128,1024]{1,0:T(8,128)}) %all-reduce.26.cloned.1.call-update) | async-done | bytes 524304
  939.2 4.3 fusion.6
  944.4 5.8 all-to-all-start.4
  950.9 8.9 all-to-all-done.4
  960.7 21.0 %psum.53 = f32[128,32]{1,0:T(8,128)S(1)} all-reduce(f32[128,32]{1,0:T(8,128)S(1)} %bitcast.111), channel_id=1, replica_groups=mesh['row'=32,'col'=8] {'col'}, use_global_device_ids=true, to_apply=%region_13.14 | all-reduce | flops 4096 | bytes 32768 | tf_op jit(solution)/shard_map/psum | solution.py:11
  982.5 0.8 scatter.30
  983.3 1.5 fusion.41
  984.9 144.0 %all-reduce.28.cloned.1.call-done = f32[128,1024]{1,0:T(8,128)} async-done(((f32[128,1024]{1,0:T(8,128)}), f32[128,1024]{1,0:T(8,128)}) %all-reduce.28.cloned.1.call-update) | async-done | bytes 524304
  1128.8 4.3 fusion.4
  1134.0 5.6 all-to-all-start.5
  1140.3 8.9 all-to-all-done.5
  1150.1 21.0 %psum.54 = f32[128,32]{1,0:T(8,128)S(1)} all-reduce(f32[128,32]{1,0:T(8,128)S(1)} %bitcast.112), channel_id=1, replica_groups=mesh['row'=32,'col'=8] {'col'}, use_global_device_ids=true, to_apply=%region_16.17 | all-reduce | flops 4096 | bytes 32768 | tf_op jit(solution)/shard_map/psum | solution.py:11
  1172.7 1.5 fusion.42
  1174.3 144.0 %all-reduce.30.cloned.1.call-done = f32[128,1024]{1,0:T(8,128)} async-done(((f32[128,1024]{1,0:T(8,128)}), f32[128,1024]{1,0:T(8,128)}) %all-reduce.30.cloned.1.call-update) | async-done | bytes 524304
  1318.3 4.3 fusion.2
  1323.4 5.6 all-to-all-start.6
  1329.8 8.9 all-to-all-done.6
  1339.5 21.3 %psum.55 = f32[128,32]{1,0:T(8,128)S(1)} all-reduce(f32[128,32]{1,0:T(8,128)S(1)} %bitcast.113), channel_id=1, replica_groups=mesh['row'=32,'col'=8] {'col'}, use_global_device_ids=true, to_apply=%region_19.20 | all-reduce | flops 4096 | bytes 32768 | tf_op jit(solution)/shard_map/psum | solution.py:11
  1362.4 1.5 fusion.43
  1364.0 143.9 %all-reduce.32.cloned.1.call-done = f32[128,1024]{1,0:T(8,128)} async-done(((f32[128,1024]{1,0:T(8,128)}), f32[128,1024]{1,0:T(8,128)}) %all-reduce.32.cloned.1.call-update) | async-done | bytes 524304
  1507.9 4.9 fusion.16
  (90 shorter events, 28.1 us)
Async XLA Ops:
  6.5 176.2 %all-reduce.18.cloned.1.call-start = ((), (), s32[]{:S(2)}) async-start(), calls=%async_computation.7 | async-start | bytes 1048576
  22.5 8.7 copy-start.2
  22.5 160.3 %copy-start.1 = (f32[4,1024]{1,0:T(4,128)S(1)}, f32[4,1024]{1,0:T(4,128)}, u32[]{:S(2)}) copy-start(f32[4,1024]{1,0:T(4,128)} %param.27) | copy-start | bytes 49156
  25.3 168.9 %copy-start = (f32[8,32,1024]{2,1,0:T(8,128)S(1)}, f32[8,32,1024]{2,1,0:T(8,128)}, u32[]{:S(2)}) copy-start(f32[8,32,1024]{2,1,0:T(8,128)} %param.25) | copy-start | bytes 3145732
  188.7 15.2 %all-to-all-start = ((f32[32,1,128]{2,1,0:T(1,128)}), f32[32,1,128]{2,1,0:T(1,128)S(1)}, u32[]{:S(2)}, u32[]{:S(2)}) async-start(f32[32,1,128]{2,1,0:T(1,128)} %reshape.244), calls=%async_computation | async-start | bytes 32768 | tf_op jit(solution)/shard_map/all_to_all | solution.py:50
  194.2 177.7 %all-reduce.20.cloned.1.call-start = ((), (), s32[]{:S(2)}) async-start(), calls=%async_computation.8 | async-start | bytes 1048576
  377.1 15.2 %all-to-all-start.1 = ((f32[32,1,128]{2,1,0:T(1,128)}), f32[32,1,128]{2,1,0:T(1,128)S(1)}, u32[]{:S(2)}, u32[]{:S(2)}) async-start(f32[32,1,128]{2,1,0:T(1,128)} %reshape.246), calls=%async_computation.1 | async-start | bytes 32768 | tf_op jit(solution)/shard_map/all_to_all | solution.py:50
  382.7 178.6 %all-reduce.22.cloned.1.call-start = ((), (), s32[]{:S(2)}) async-start(), calls=%async_computation.9 | async-start | bytes 1048576
  566.4 15.2 %all-to-all-start.2 = ((f32[32,1,128]{2,1,0:T(1,128)}), f32[32,1,128]{2,1,0:T(1,128)S(1)}, u32[]{:S(2)}, u32[]{:S(2)}) async-start(f32[32,1,128]{2,1,0:T(1,128)} %reshape.248), calls=%async_computation.2 | async-start | bytes 32768 | tf_op jit(solution)/shard_map/all_to_all | solution.py:50
  571.9 178.4 %all-reduce.24.cloned.1.call-start = ((), (), s32[]{:S(2)}) async-start(), calls=%async_computation.10 | async-start | bytes 1048576
  755.5 15.2 %all-to-all-start.3 = ((f32[32,1,128]{2,1,0:T(1,128)}), f32[32,1,128]{2,1,0:T(1,128)S(1)}, u32[]{:S(2)}, u32[]{:S(2)}) async-start(f32[32,1,128]{2,1,0:T(1,128)} %reshape.250), calls=%async_computation.3 | async-start | bytes 32768 | tf_op jit(solution)/shard_map/all_to_all | solution.py:50
  761.1 178.2 %all-reduce.26.cloned.1.call-start = ((), (), s32[]{:S(2)}) async-start(), calls=%async_computation.11 | async-start | bytes 1048576
  944.4 15.5 %all-to-all-start.4 = ((f32[32,1,128]{2,1,0:T(1,128)}), f32[32,1,128]{2,1,0:T(1,128)S(1)}, u32[]{:S(2)}, u32[]{:S(2)}) async-start(f32[32,1,128]{2,1,0:T(1,128)} %reshape.252), calls=%async_computation.4 | async-start | bytes 32768 | tf_op jit(solution)/shard_map/all_to_all | solution.py:50
  950.2 178.7 %all-reduce.28.cloned.1.call-start = ((), (), s32[]{:S(2)}) async-start(), calls=%async_computation.12 | async-start | bytes 1048576
  1134.0 15.2 %all-to-all-start.5 = ((f32[32,1,128]{2,1,0:T(1,128)}), f32[32,1,128]{2,1,0:T(1,128)S(1)}, u32[]{:S(2)}, u32[]{:S(2)}) async-start(f32[32,1,128]{2,1,0:T(1,128)} %reshape.254), calls=%async_computation.5 | async-start | bytes 32768 | tf_op jit(solution)/shard_map/all_to_all | solution.py:50
  1139.5 178.7 %all-reduce.30.cloned.1.call-start = ((), (), s32[]{:S(2)}) async-start(), calls=%async_computation.13 | async-start | bytes 1048576
  1323.4 15.2 %all-to-all-start.6 = ((f32[32,1,128]{2,1,0:T(1,128)}), f32[32,1,128]{2,1,0:T(1,128)S(1)}, u32[]{:S(2)}, u32[]{:S(2)}) async-start(f32[32,1,128]{2,1,0:T(1,128)} %reshape.256), calls=%async_computation.6 | async-start | bytes 32768 | tf_op jit(solution)/shard_map/all_to_all | solution.py:50
  1329.0 178.9 %all-reduce.32.cloned.1.call-start = ((), (), s32[]{:S(2)}) async-start(), calls=%async_computation.14 | async-start | bytes 1048576
Sparse Core Ops, SparseCore 0:
  31.3 151.4 all-reduce.17
  228.0 143.8 all-reduce.19
  417.4 143.8 all-reduce.21
  606.5 143.7 all-reduce.23
  795.4 143.7 all-reduce.25
  985.0 143.7 all-reduce.27
  1174.4 143.8 all-reduce.29
  1364.1 143.7 all-reduce.31
where the time goes:
time: 1520 us
  waiting for transfers between devices  1220 us (80%)
  blocking collectives  161 us (11%)
  matrix products  51.4 us (3%)
  starting transfers between devices  39.4 us (3%)
  other arithmetic  16.3 us (1%)
  between operations  15.4 us (1%)
    unnamed x16, waiting for transfers between devices  1160 us
    psum x7, blocking collectives, broadcast(): return lax.psum(jnp.where(mine, array, jnp.zeros_like(array)), axis)  147 us
    all_to_all x7, waiting for transfers between devices, on_device(): lax.all_to_all(solved, 'row', split_axis=1, concat_axis=0, tiled=True)  62.8 us
    all_to_all x7, starting transfers between devices, on_device(): lax.all_to_all(solved, 'row', split_axis=1, concat_axis=0, tiled=True)  39.1 us
    dot_general x8, matrix products, on_device(): jnp.dot(reduced - pending, diag_inverse[0], precision=highest, preferred_...  34.9 us
  transfers between devices with their start and end apart: 15, of which 15 were waited for; matrix products, arithmetic and copies ran while one was open for 0% of the time, Pallas kernels for 0%

commit v1 on v0

--- a/solution.py
+++ b/solution.py
@@ -8,7 +8,7 @@
 
 def broadcast(array, axis, root):
     mine = lax.axis_index(axis) == root
-    return lax.psum(jnp.where(mine, array, jnp.zeros_like(array)), axis)
+    return jnp.sum(lax.all_gather(jnp.where(mine, array, jnp.zeros_like(array)), axis), axis=0)
 
 
 def on_device(anc_factor, anc_solution, slot_row, tile_count, lower_factor, diag_inverse, rhs):

time: 1520 us -> 1450 us (0.954)
  blocking collectives: 161 us -> 103 us
    psum x7 -> x0, blocking collectives: 147 us -> none  [broadcast(): return lax.psum(jnp.where(mine, array, jnp.zeros_like(array)), axis)]
    all_gather x0 -> x7, blocking collectives: none -> 89.7 us  [broadcast(): lax.all_gather(jnp.where(mine, array, jnp.zeros_like(array)), axis)]
where the time goes in v1:
time: 1450 us
  waiting for transfers between devices  1220 us (84%)
  blocking collectives  103 us (7%)
  matrix products  51.3 us (4%)
  starting transfers between devices  39.4 us (3%)
  other arithmetic  16.1 us (1%)
  between operations  15.3 us (1%)
    unnamed x16, waiting for transfers between devices  1150 us
    all_gather x7, blocking collectives, broadcast(): lax.all_gather(jnp.where(mine, array, jnp.zeros_like(array)), axis)  89.7 us
    all_to_all x7, waiting for transfers between devices, on_device(): lax.all_to_all(solved, 'row', split_axis=1, concat_axis=0, tiled=True)  62.9 us
    all_to_all x7, starting transfers between devices, on_device(): lax.all_to_all(solved, 'row', split_axis=1, concat_axis=0, tiled=True)  39.1 us
    dot_general x8, matrix products, on_device(): jnp.dot(reduced - pending, diag_inverse[0], precision=highest, preferred_...  34.9 us
  transfers between devices with their start and end apart: 15, of which 15 were waited for; matrix products, arithmetic and copies ran while one was open for 0% of the time, Pallas kernels for 0%

profile of v1, /device:TPU:2, one launch (start us, length us, event | category | flops | bytes accessed | tf_op | source)
XLA Modules:
  0.0 1452.2 jit_solution(14312488459196534371)
XLA Ops:
  8.6 13.7 all_gather.31
  22.5 2.8 gather_fusion
  25.3 5.8 fusion.19
  32.4 150.3 %all-reduce.18.cloned.1.call-done = f32[128,1024]{1,0:T(8,128)} async-done(((f32[128,1024]{1,0:T(8,128)}), f32[128,1024]{1,0:T(8,128)}) %all-reduce.18.cloned.1.call-update) | async-done | bytes 524304
  182.8 0.8 dynamic-slice_subtract_fusion.14
  183.5 4.3 fusion.14
  188.7 5.6 all-to-all-start
  194.5 9.4 all-to-all-done
  205.4 12.8 all_gather.32
  218.2 1.5 fusion.25
  219.7 143.2 %all-reduce.20.cloned.1.call-done = f32[128,1024]{1,0:T(8,128)} async-done(((f32[128,1024]{1,0:T(8,128)}), f32[128,1024]{1,0:T(8,128)}) %all-reduce.20.cloned.1.call-update) | async-done | bytes 524304
  362.9 4.3 fusion.12
  368.1 5.6 all-to-all-start.1
  374.4 8.9 all-to-all-done.1
  384.2 12.9 all_gather.33
  397.9 1.5 fusion.43
  399.4 143.1 %all-reduce.22.cloned.1.call-done = f32[128,1024]{1,0:T(8,128)} async-done(((f32[128,1024]{1,0:T(8,128)}), f32[128,1024]{1,0:T(8,128)}) %all-reduce.22.cloned.1.call-update) | async-done | bytes 524304
  542.6 4.3 fusion.10
  547.7 5.6 all-to-all-start.2
  554.0 8.9 all-to-all-done.2
  563.9 12.8 all_gather.34
  577.3 1.5 fusion.44
  578.9 143.1 %all-reduce.24.cloned.1.call-done = f32[128,1024]{1,0:T(8,128)} async-done(((f32[128,1024]{1,0:T(8,128)}), f32[128,1024]{1,0:T(8,128)}) %all-reduce.24.cloned.1.call-update) | async-done | bytes 524304
  722.0 4.3 fusion.8
  727.2 5.6 all-to-all-start.3
  733.5 8.9 all-to-all-done.3
  743.3 12.8 all_gather.35
  756.8 1.5 fusion.45
  758.3 143.1 %all-reduce.26.cloned.1.call-done = f32[128,1024]{1,0:T(8,128)} async-done(((f32[128,1024]{1,0:T(8,128)}), f32[128,1024]{1,0:T(8,128)}) %all-reduce.26.cloned.1.call-update) | async-done | bytes 524304
  901.5 4.3 fusion.6
  906.6 5.8 all-to-all-start.4
  913.2 8.9 all-to-all-done.4
  923.0 12.8 all_gather.36
  936.5 1.5 fusion.46
  938.0 143.1 %all-reduce.28.cloned.1.call-done = f32[128,1024]{1,0:T(8,128)} async-done(((f32[128,1024]{1,0:T(8,128)}), f32[128,1024]{1,0:T(8,128)}) %all-reduce.28.cloned.1.call-update) | async-done | bytes 524304
  1081.2 4.3 fusion.4
  1086.3 5.6 all-to-all-start.5
  1092.6 8.9 all-to-all-done.5
  1102.5 12.8 all_gather.37
  1115.9 1.5 fusion.47
  1117.5 143.2 %all-reduce.30.cloned.1.call-done = f32[128,1024]{1,0:T(8,128)} async-done(((f32[128,1024]{1,0:T(8,128)}), f32[128,1024]{1,0:T(8,128)}) %all-reduce.30.cloned.1.call-update) | async-done | bytes 524304
  1260.7 4.3 fusion.2
  1265.8 5.6 all-to-all-start.6
  1272.2 8.9 all-to-all-done.6
  1282.0 13.0 all_gather.38
  1295.7 1.5 fusion.48
  1297.3 143.1 %all-reduce.32.cloned.1.call-done = f32[128,1024]{1,0:T(8,128)} async-done(((f32[128,1024]{1,0:T(8,128)}), f32[128,1024]{1,0:T(8,128)}) %all-reduce.32.cloned.1.call-update) | async-done | bytes 524304
  1440.4 4.9 fusion.16
  (98 shorter events, 24.2 us)
Async XLA Ops:
  6.5 176.2 %all-reduce.18.cloned.1.call-start = ((), (), s32[]{:S(2)}) async-start(), calls=%async_computation.7 | async-start | bytes 1048576
  22.5 8.7 copy-start.2
  22.5 160.3 %copy-start.1 = (f32[4,1024]{1,0:T(4,128)S(1)}, f32[4,1024]{1,0:T(4,128)}, u32[]{:S(2)}) copy-start(f32[4,1024]{1,0:T(4,128)} %param.27) | copy-start | bytes 49156
  25.3 168.9 %copy-start = (f32[8,32,1024]{2,1,0:T(8,128)S(1)}, f32[8,32,1024]{2,1,0:T(8,128)}, u32[]{:S(2)}) copy-start(f32[8,32,1024]{2,1,0:T(8,128)} %param.25) | copy-start | bytes 3145732
  188.7 15.2 %all-to-all-start = ((f32[32,1,128]{2,1,0:T(1,128)}), f32[32,1,128]{2,1,0:T(1,128)S(1)}, u32[]{:S(2)}, u32[]{:S(2)}) async-start(f32[32,1,128]{2,1,0:T(1,128)} %reshape.314), calls=%async_computation | async-start | bytes 32768 | tf_op jit(solution)/shard_map/all_to_all | solution.py:50
  194.2 168.7 %all-reduce.20.cloned.1.call-start = ((), (), s32[]{:S(2)}) async-start(), calls=%async_computation.8 | async-start | bytes 1048576
  368.1 15.2 %all-to-all-start.1 = ((f32[32,1,128]{2,1,0:T(1,128)}), f32[32,1,128]{2,1,0:T(1,128)S(1)}, u32[]{:S(2)}, u32[]{:S(2)}) async-start(f32[32,1,128]{2,1,0:T(1,128)} %reshape.316), calls=%async_computation.1 | async-start | bytes 32768 | tf_op jit(solution)/shard_map/all_to_all | solution.py:50
  373.6 168.9 %all-reduce.22.cloned.1.call-start = ((), (), s32[]{:S(2)}) async-start(), calls=%async_computation.9 | async-start | bytes 1048576
  547.7 15.2 %all-to-all-start.2 = ((f32[32,1,128]{2,1,0:T(1,128)}), f32[32,1,128]{2,1,0:T(1,128)S(1)}, u32[]{:S(2)}, u32[]{:S(2)}) async-start(f32[32,1,128]{2,1,0:T(1,128)} %reshape.318), calls=%async_computation.2 | async-start | bytes 32768 | tf_op jit(solution)/shard_map/all_to_all | solution.py:50
  553.3 168.8 %all-reduce.24.cloned.1.call-start = ((), (), s32[]{:S(2)}) async-start(), calls=%async_computation.10 | async-start | bytes 1048576
  727.2 15.2 %all-to-all-start.3 = ((f32[32,1,128]{2,1,0:T(1,128)}), f32[32,1,128]{2,1,0:T(1,128)S(1)}, u32[]{:S(2)}, u32[]{:S(2)}) async-start(f32[32,1,128]{2,1,0:T(1,128)} %reshape.320), calls=%async_computation.3 | async-start | bytes 32768 | tf_op jit(solution)/shard_map/all_to_all | solution.py:50
  732.7 168.8 %all-reduce.26.cloned.1.call-start = ((), (), s32[]{:S(2)}) async-start(), calls=%async_computation.11 | async-start | bytes 1048576
  906.6 15.5 %all-to-all-start.4 = ((f32[32,1,128]{2,1,0:T(1,128)}), f32[32,1,128]{2,1,0:T(1,128)S(1)}, u32[]{:S(2)}, u32[]{:S(2)}) async-start(f32[32,1,128]{2,1,0:T(1,128)} %reshape.322), calls=%async_computation.4 | async-start | bytes 32768 | tf_op jit(solution)/shard_map/all_to_all | solution.py:50
  912.4 168.8 %all-reduce.28.cloned.1.call-start = ((), (), s32[]{:S(2)}) async-start(), calls=%async_computation.12 | async-start | bytes 1048576
  1086.3 15.2 %all-to-all-start.5 = ((f32[32,1,128]{2,1,0:T(1,128)}), f32[32,1,128]{2,1,0:T(1,128)S(1)}, u32[]{:S(2)}, u32[]{:S(2)}) async-start(f32[32,1,128]{2,1,0:T(1,128)} %reshape.324), calls=%async_computation.5 | async-start | bytes 32768 | tf_op jit(solution)/shard_map/all_to_all | solution.py:50
  1091.9 168.8 %all-reduce.30.cloned.1.call-start = ((), (), s32[]{:S(2)}) async-start(), calls=%async_computation.13 | async-start | bytes 1048576
  1265.8 15.2 %all-to-all-start.6 = ((f32[32,1,128]{2,1,0:T(1,128)}), f32[32,1,128]{2,1,0:T(1,128)S(1)}, u32[]{:S(2)}, u32[]{:S(2)}) async-start(f32[32,1,128]{2,1,0:T(1,128)} %reshape.326), calls=%async_computation.6 | async-start | bytes 32768 | tf_op jit(solution)/shard_map/all_to_all | solution.py:50
  1271.4 169.0 %all-reduce.32.cloned.1.call-start = ((), (), s32[]{:S(2)}) async-start(), calls=%async_computation.14 | async-start | bytes 1048576
Sparse Core Ops, SparseCore 0:
  31.3 151.4 all-reduce.17
  219.8 143.0 all-reduce.19
  399.5 142.9 all-reduce.21
  579.0 142.9 all-reduce.23
  758.5 142.9 all-reduce.25
  938.2 142.9 all-reduce.27
  1117.6 143.0 all-reduce.29
  1297.4 142.9 all-reduce.31
